TPU v7x, 32 devices: a whole 2x2x4 slice. The times are simulated.
32 devices in a mesh: groups: 2 (over y), seq: 4 (over z), adapt: 4 (over x, core).
Axes of the slice: x: 2, y: 2, z: 4, core: 2. Of those that a mesh axis runs over, the one named last changes fastest.
Arguments:
- image: bfloat16 [16, 2048, 3072], P(('groups', 'adapt'), 'seq'), parts along dimension 0, may hold values from -6 to 6
- modulation: float32 [16, 2, 3072], P(('groups', 'adapt')), parts along dimension 0, may hold values from -3 to 3
- query_key_value_weight: bfloat16 [3072, 6144], P(None, 'adapt'), may hold values from -0.109375 to 0.109375
- pooled_down_factor: bfloat16 [16, 3072, 64], P('seq'), may hold values from -0.109375 to 0.109375
- pooled_up_factor: bfloat16 [16, 64, 6144], P('seq', None, 'adapt'), may hold values from -0.75 to 0.75
- request_adapter: int32 [16], P('groups'), parts along dimension 0, may hold values from 0 to 15
- adapter_slot_table: int32 [16], replicated, may hold values from 0 to 15, each once
- row_request: int32 [16], P('groups'), parts along dimension 0, may hold values from 0 to 7, each once
- text_key_value: bfloat16 [16, 512, 2, 2048], P('groups', 'seq', None, 'adapt'), parts along dimension 0, may hold values from -110 to 110
- query_key_gain: float32 [2, 128], replicated, may hold values from 1 to 2.5
Outputs:
- attended: bfloat16 [16, 2048, 2048], P('groups', 'seq', 'adapt'), parts along dimension 0
There are 2 independent parts, one for each index of `groups`. A program takes and returns all parts, laid end to end along the dimension named above; an argument that names none is the same for every part. Nothing has to cross between parts.
All inputs are finite; a program needn't handle non-finite values.
Results may differ from a plain program's by a relative error of at most 0.0049.
The roundings to bfloat16 on the way count: a program that leaves them out, or rounds other values in their place, can miss the bound.
Values may be sent and summed in bfloat16 or wider, within the bound.
A program may use at most 192 MiB of HBM per device.

v0:
```python
import math
import jax
import jax.numpy as jnp
from jax import lax
from jax.sharding import PartitionSpec as P

HEAD_SIZE = 128


def layer_modulate(image, modulation):
    widened = image.astype(jnp.float32)
    centre = widened - jnp.mean(widened, axis=-1, keepdims=True)
    variance = jnp.mean(centre * centre, axis=-1, keepdims=True)
    normed = centre * lax.rsqrt(variance + 1e-06)
    return ((1.0 + modulation[:, 1, None, :]) * normed + modulation[:, 0, None, :]).astype(
        jnp.bfloat16
    )


def rms_scale(values, gain):
    return values * lax.rsqrt(jnp.mean(values * values, axis=-1, keepdims=True) + 1e-06) * gain


def attend_item(operands):
    queries, joined = operands
    key_rows = joined[:, 0]
    value_rows = joined[:, 1]
    query_count = queries.shape[0]
    block = math.gcd(query_count, 512)
    inverse = 1.0 / math.sqrt(queries.shape[-1])
    blocked = queries.reshape(query_count // block, block, queries.shape[-1])

    def one_block(block_rows):
        scores = (
            lax.dot_general(
                block_rows, key_rows, (((1,), (1,)), ((), ())), preferred_element_type=jnp.float32
            )
            * inverse
        )
        highest = jnp.max(scores, axis=-1, keepdims=True)
        weights = jnp.exp(scores - highest)
        weights = weights / jnp.sum(weights, axis=-1, keepdims=True)
        return jnp.dot(
            weights.astype(jnp.bfloat16), value_rows, preferred_element_type=jnp.float32
        ).astype(jnp.bfloat16)

    return lax.map(one_block, blocked).reshape(queries.shape)


def on_device(
    image,
    modulation,
    query_key_value_weight,
    pooled_down_factor,
    pooled_up_factor,
    request_adapter,
    adapter_slot_table,
    row_request,
    text_key_value,
    query_key_gain,
):
    seq_index = lax.axis_index("seq")
    all_requests = request_adapter.shape[0]
    local_pool_slice = pooled_down_factor.shape[0]
    pool_total = adapter_slot_table.shape[0]
    heads_local = query_key_value_weight.shape[1] // (3 * HEAD_SIZE)
    text_local = text_key_value.shape[1]
    modulated = layer_modulate(image, modulation)
    request_match = row_request[:, None] == jnp.arange(all_requests, dtype=jnp.int32)[None, :]
    chosen_ids = jnp.sum(jnp.where(request_match, request_adapter[None, :], 0), axis=1)
    slot_match = chosen_ids[:, None] == jnp.arange(pool_total, dtype=jnp.int32)[None, :]
    slots = jnp.sum(jnp.where(slot_match, adapter_slot_table[None, :], 0), axis=1)
    owned = slots // local_pool_slice == seq_index
    local_match = (slots % local_pool_slice)[:, None] == jnp.arange(
        local_pool_slice, dtype=jnp.int32
    )[None, :]
    slot_picker = (owned[:, None] & local_match).astype(jnp.bfloat16)
    up_terms = jnp.einsum(
        "eq,qfx->efx", slot_picker, pooled_up_factor, preferred_element_type=jnp.float32
    ).astype(jnp.bfloat16)
    down_terms = jnp.einsum(
        "mv,vna->mna", slot_picker, pooled_down_factor, preferred_element_type=jnp.float32
    ).astype(jnp.bfloat16)
    down_fetched, up_fetched = (
        lax.psum(down_terms, "seq").astype(jnp.float32),
        lax.psum(up_terms, "seq").astype(jnp.float32),
    )
    down_fetched = down_fetched.astype(jnp.bfloat16)
    up_fetched = up_fetched.astype(jnp.bfloat16)
    block_rows = lax.all_gather(modulated, "adapt", axis=0, tiled=True)
    shrunk = jnp.einsum(
        "rtd,rdk->rtk", block_rows, down_fetched, preferred_element_type=jnp.float32
    ).astype(jnp.bfloat16)
    frozen = jnp.einsum(
        "rtd,dc->rtc", block_rows, query_key_value_weight, preferred_element_type=jnp.float32
    )
    qkv = frozen + jnp.einsum(
        "rtk,rkc->rtc", shrunk, up_fetched, preferred_element_type=jnp.float32
    )
    token_local = qkv.shape[1]
    qkv = qkv.reshape(all_requests, token_local, heads_local, 3, HEAD_SIZE)
    queries = rms_scale(qkv[:, :, :, 0], query_key_gain[0]).astype(jnp.bfloat16)
    image_keys = rms_scale(qkv[:, :, :, 1], query_key_gain[1]).astype(jnp.bfloat16)
    image_values = qkv[:, :, :, 2].astype(jnp.bfloat16)
    image_pairs = jnp.transpose(jnp.stack([image_keys, image_values], axis=3), (0, 2, 1, 3, 4))
    text_pairs = jnp.transpose(
        text_key_value.reshape(all_requests, text_local, 2, heads_local, HEAD_SIZE), (0, 3, 1, 2, 4)
    )
    joined = jnp.concatenate([image_pairs, text_pairs], axis=2)
    joined = joined.reshape(all_requests * heads_local, token_local + text_local, 2, HEAD_SIZE)
    queries = jnp.transpose(queries, (0, 2, 1, 3)).reshape(
        all_requests * heads_local, token_local, HEAD_SIZE
    )
    query_items, joined_items = (
        lax.all_to_all(queries, "seq", split_axis=0, concat_axis=1, tiled=True),
        lax.all_to_all(joined, "seq", split_axis=0, concat_axis=1, tiled=True),
    )
    attended = lax.map(attend_item, (query_items, joined_items))
    returned = lax.all_to_all(attended, "seq", split_axis=1, concat_axis=0, tiled=True)
    returned = returned.reshape(all_requests, heads_local, token_local, HEAD_SIZE)
    return jnp.transpose(returned, (0, 2, 1, 3)).reshape(
        all_requests, token_local, heads_local * HEAD_SIZE
    )


def solution(mesh):
    in_specs = (
        P(("groups", "adapt"), "seq", None),
        P(("groups", "adapt"), None, None),
        P(None, "adapt"),
        P("seq", None, None),
        P("seq", None, "adapt"),
        P("groups"),
        P(),
        P("groups"),
        P("groups", "seq", None, "adapt"),
        P(),
    )
    out_specs = P("groups", "seq", "adapt")
    return jax.shard_map(
        on_device, mesh=mesh, in_specs=in_specs, out_specs=out_specs, check_vma=False
    )
```

profile of v0, /device:TPU:0, one launch (start us, length us, event | category | flops | bytes accessed | tf_op | source)
XLA Modules:
  0.0 888.3 jit_solution(3175267230559958143)
XLA Ops:
  9.2 2.8 convolution_convert_fusion
  12.1 3.1 convolution_convert_fusion.1
  15.2 3.7 convert_reduce_fusion
  18.9 4.5 fusion.10
  23.6 9.4 %fusion.13 = bf16[2,512,3072]{2,1,0:T(8,128)(2,1)} fusion(bf16[2,512,3072]{2,1,0:T(8,128)(2,1)} %param.14, f32[2,3072]{1,0:T(2,128)S(1)} %get-tuple-element.83, f32[2,512]{1,0:T(2,128)S(1)} %add_rsqrt_fusion.2, f32[2,512]{1,0:T(2,128)S(1)} %broadcast_multiply_fusion, f32[2,3072]{1,0:T(2,128)S(1)} %get-tuple-element.84), kind=kLoop, calls=%fused_computation.24 | loop fusion | flops 18874368 | bytes 12640256 | tf_op jit(solution)/shard_map/convert_element_type | solution.py:15
  34.2 156.1 %all-reduce.3.cloned.1.call-done = (bf16[8,64,1536]{2,0,1:T(8,128)(2,1)}, bf16[8,3072,64]{1,0,2:T(8,128)(2,1)}) async-done(((bf16[8,64,1536]{2,0,1:T(8,128)(2,1)}, bf16[8,3072,64]{1,0,2:T(8,128)(2,1)}), (bf16[8,64,1536]{2,0,1:T(8,128)(2,1)}, bf16[8,3072,64]{1,0,2:T(8,128)(2,1)})) %all-reduce.3.cloned.1.call-update) | async-done | bytes 4718608 | tf_op jit(solution)/shard_map/psum | solution.py:86
  190.3 23.9 %fusion.18 = f32[8,512,1536]{2,1,0:T(8,128)} fusion(bf16[8,64,1536]{2,0,1:T(8,128)(2,1)} %get-tuple-element.73, bf16[8,512,3072]{2,1,0:T(8,128)(2,1)} %all-gather.2.cloned.1.call-done, bf16[8,3072,64]{1,0,2:T(8,128)(2,1)} %get-tuple-element.74), kind=kOutput, calls=%fused_computation.40 | convolution fusion | flops 2416181248 | bytes 55050240 | tf_op jit(solution)/shard_map/rtk,rkc->rtc/dot_general | solution.py:97
  214.3 47.6 %convolution_add_fusion = f32[8,512,1536]{2,1,0:T(8,128)} fusion(f32[8,512,1536]{2,1,0:T(8,128)} %fusion.18, bf16[8,512,3072]{2,1,0:T(8,128)(2,1)} %all-gather.2.cloned.1.call-done, bf16[3072,1536]{1,0:T(8,128)(2,1)} %param.16), kind=kOutput, calls=%fused_computation.16 | convolution fusion | flops 38660997120 | bytes 84934656 | tf_op jit(solution)/shard_map/rtd,dc->rtc/dot_general | solution.py:94
  261.9 24.7 %copy.49 = f32[8,512,1536]{1,2,0:T(8,128)} copy(f32[8,512,1536]{2,1,0:T(8,128)} %convolution_add_fusion) | data formatting | bytes 50331648 | tf_op jit(solution)/shard_map/add | solution.py:97
  286.6 4.6 multiply_reduce_fusion.1
  291.2 7.0 fusion.15
  298.2 6.5 copy.50
  304.6 5.2 all-to-all-start
  309.8 6.2 copy.52
  316.0 3.2 copy.79
  319.1 4.0 slice.55
  323.1 4.6 multiply_reduce_fusion
  327.8 7.0 multiply_convert_fusion
  334.7 6.2 maximum_bitcast_fusion
  340.9 9.1 %pad_maximum_fusion = bf16[8,4,640,2,128]{2,4,3,1,0:T(8,128)(2,1)} fusion(bf16[8,4,128,2,128]{2,4,3,1,0:T(8,128)(2,1)} %bitcast.102, bf16[8,4,512,2,128]{2,4,3,1,0:T(8,128)(2,1)} %maximum_bitcast_fusion), kind=kLoop, calls=%fused_computation.25 | loop fusion | flops 20971520 | bytes 20971520 | tf_op jit(solution)/shard_map/concatenate | solution.py:109
  350.1 15.1 %copy.54 = bf16[8,4,640,2,128]{4,2,3,1,0:T(8,128)(2,1)} copy(bf16[8,4,640,2,128]{2,4,3,1,0:T(8,128)(2,1)} %pad_maximum_fusion) | data formatting | bytes 20971520 | tf_op jit(solution)/shard_map/concatenate | solution.py:109
  365.2 38.2 %all-to-all-done = bf16[32,512,128]{2,1,0:T(8,128)(2,1)} async-done(((bf16[32,512,128]{2,1,0:T(8,128)(2,1)}), bf16[32,512,128]{2,1,0:T(8,128)(2,1)}, u32[]{:S(2)}, u32[]{:S(2)}) %all-to-all-start) | async-done | bytes 4194336 | tf_op jit(solution)/shard_map/all_to_all | solution.py:115
  403.3 6.0 all-to-all-start.1
  409.4 4.6 copy.51
  414.0 223.2 %all-to-all-done.1 = bf16[32,640,2,128]{3,1,2,0:T(8,128)(2,1)} async-done(((bf16[32,640,2,128]{3,1,2,0:T(8,128)(2,1)}), bf16[32,640,2,128]{3,1,2,0:T(8,128)(2,1)}, u32[]{:S(2)}, u32[]{:S(2)}) %all-to-all-start.1) | async-done | bytes 10485792 | tf_op jit(solution)/shard_map/all_to_all | solution.py:116
  637.1 9.2 %copy.55 = bf16[8,4,640,2,128]{4,2,1,3,0:T(8,128)(2,1)} copy(bf16[8,4,640,2,128]{4,2,3,0,1:T(8,128)(2,1)} %bitcast.23) | data formatting | bytes 20971520 | tf_op jit(solution)/shard_map/all_to_all | solution.py:116
  646.3 118.3 %while.21 = (s32[]{:T(128)}, bf16[8,2048,128]{2,1,0:T(8,128)(2,1)}, bf16[8,2048,128]{2,1,0:T(8,128)(2,1)}, bf16[8,2560,2,128]{3,1,2,0:T(8,128)(2,1)}, s32[]{:T(128)}, /*index=5*/s32[]{:T(128)}, s32[]{:T(128)}) while((s32[]{:T(128)}, bf16[8,2048,128]{2,1,0:T(8,128)(2,1)}, bf16[8,2048,128]{2,1,0:T(8,128)(2,1)}, ...), condition=%wide.region_13.14_spmd, body=%wide.region_8.13_spmd.sunk | while | flops 680328192 | bytes 24652504 | solution.py:118
  646.3 1.4 dynamic-slice_bitcast_fusion.2
  647.8 1.1 constant_dynamic-slice_fusion.2
  648.9 11.3 %while.22 = (s32[]{:T(128)}, bf16[4,512,128]{2,1,0:T(8,128)(2,1)S(1)}, bf16[4,512,128]{2,1,0:T(8,128)(2,1)S(1)}, bf16[2560,128]{1,0:T(8,128)(2,1)S(1)}, bf16[2560,128]{1,0:T(8,128)(2,1)S(1)}, /*index=5*/s32[]{:T(128)}) while((s32[]{:T(128)}, bf16[4,512,128]{2,1,0:T(8,128)(2,1)S(1)}, bf16[4,512,128]{2,1,0:T(8,128)(2,1)S(1)}, ...), condition=%wide.region_12.12_spmd, body=%wide.region_9.11_spmd.sunk | while | flops 680328192 | bytes 17311820 | solution.py:47
  653.6 1.0 fusion.46
  656.4 1.0 fusion.46
  659.2 1.0 fusion.46
  661.1 1.4 dynamic-slice_bitcast_fusion.2
  662.6 1.1 constant_dynamic-slice_fusion.2
  663.7 11.4 %while.22 = (s32[]{:T(128)}, bf16[4,512,128]{2,1,0:T(8,128)(2,1)S(1)}, bf16[4,512,128]{2,1,0:T(8,128)(2,1)S(1)}, bf16[2560,128]{1,0:T(8,128)(2,1)S(1)}, bf16[2560,128]{1,0:T(8,128)(2,1)S(1)}, /*index=5*/s32[]{:T(128)}) while((s32[]{:T(128)}, bf16[4,512,128]{2,1,0:T(8,128)(2,1)S(1)}, bf16[4,512,128]{2,1,0:T(8,128)(2,1)S(1)}, ...), condition=%wide.region_12.12_spmd, body=%wide.region_9.11_spmd.sunk | while | flops 680328192 | bytes 17311820 | solution.py:47
  668.3 1.0 fusion.46
  671.2 1.0 fusion.46
  674.0 1.0 fusion.46
  675.9 1.4 dynamic-slice_bitcast_fusion.2
  677.4 1.1 constant_dynamic-slice_fusion.2
  678.5 11.4 %while.22 = (s32[]{:T(128)}, bf16[4,512,128]{2,1,0:T(8,128)(2,1)S(1)}, bf16[4,512,128]{2,1,0:T(8,128)(2,1)S(1)}, bf16[2560,128]{1,0:T(8,128)(2,1)S(1)}, bf16[2560,128]{1,0:T(8,128)(2,1)S(1)}, /*index=5*/s32[]{:T(128)}) while((s32[]{:T(128)}, bf16[4,512,128]{2,1,0:T(8,128)(2,1)S(1)}, bf16[4,512,128]{2,1,0:T(8,128)(2,1)S(1)}, ...), condition=%wide.region_12.12_spmd, body=%wide.region_9.11_spmd.sunk | while | flops 680328192 | bytes 17311820 | solution.py:47
  680.3 1.0 fusion.46
  683.1 1.0 fusion.46
  690.7 1.4 dynamic-slice_bitcast_fusion.2
  692.2 1.1 constant_dynamic-slice_fusion.2
  693.3 11.4 %while.22 = (s32[]{:T(128)}, bf16[4,512,128]{2,1,0:T(8,128)(2,1)S(1)}, bf16[4,512,128]{2,1,0:T(8,128)(2,1)S(1)}, bf16[2560,128]{1,0:T(8,128)(2,1)S(1)}, bf16[2560,128]{1,0:T(8,128)(2,1)S(1)}, /*index=5*/s32[]{:T(128)}) while((s32[]{:T(128)}, bf16[4,512,128]{2,1,0:T(8,128)(2,1)S(1)}, bf16[4,512,128]{2,1,0:T(8,128)(2,1)S(1)}, ...), condition=%wide.region_12.12_spmd, body=%wide.region_9.11_spmd.sunk | while | flops 680328192 | bytes 17311820 | solution.py:47
  705.5 1.4 dynamic-slice_bitcast_fusion.2
  707.0 1.1 constant_dynamic-slice_fusion.2
  708.1 11.4 %while.22 = (s32[]{:T(128)}, bf16[4,512,128]{2,1,0:T(8,128)(2,1)S(1)}, bf16[4,512,128]{2,1,0:T(8,128)(2,1)S(1)}, bf16[2560,128]{1,0:T(8,128)(2,1)S(1)}, bf16[2560,128]{1,0:T(8,128)(2,1)S(1)}, /*index=5*/s32[]{:T(128)}) while((s32[]{:T(128)}, bf16[4,512,128]{2,1,0:T(8,128)(2,1)S(1)}, bf16[4,512,128]{2,1,0:T(8,128)(2,1)S(1)}, ...), condition=%wide.region_12.12_spmd, body=%wide.region_9.11_spmd.sunk | while | flops 680328192 | bytes 17311820 | solution.py:47
  720.3 1.4 dynamic-slice_bitcast_fusion.2
  721.8 1.1 constant_dynamic-slice_fusion.2
  722.9 11.4 %while.22 = (s32[]{:T(128)}, bf16[4,512,128]{2,1,0:T(8,128)(2,1)S(1)}, bf16[4,512,128]{2,1,0:T(8,128)(2,1)S(1)}, bf16[2560,128]{1,0:T(8,128)(2,1)S(1)}, bf16[2560,128]{1,0:T(8,128)(2,1)S(1)}, /*index=5*/s32[]{:T(128)}) while((s32[]{:T(128)}, bf16[4,512,128]{2,1,0:T(8,128)(2,1)S(1)}, bf16[4,512,128]{2,1,0:T(8,128)(2,1)S(1)}, ...), condition=%wide.region_12.12_spmd, body=%wide.region_9.11_spmd.sunk | while | flops 680328192 | bytes 17311820 | solution.py:47
  735.1 1.4 dynamic-slice_bitcast_fusion.2
  736.6 1.1 constant_dynamic-slice_fusion.2
  737.6 11.4 %while.22 = (s32[]{:T(128)}, bf16[4,512,128]{2,1,0:T(8,128)(2,1)S(1)}, bf16[4,512,128]{2,1,0:T(8,128)(2,1)S(1)}, bf16[2560,128]{1,0:T(8,128)(2,1)S(1)}, bf16[2560,128]{1,0:T(8,128)(2,1)S(1)}, /*index=5*/s32[]{:T(128)}) while((s32[]{:T(128)}, bf16[4,512,128]{2,1,0:T(8,128)(2,1)S(1)}, bf16[4,512,128]{2,1,0:T(8,128)(2,1)S(1)}, ...), condition=%wide.region_12.12_spmd, body=%wide.region_9.11_spmd.sunk | while | flops 680328192 | bytes 17311820 | solution.py:47
  749.8 1.4 dynamic-slice_bitcast_fusion.2
  751.3 1.1 constant_dynamic-slice_fusion.2
  752.4 11.4 %while.22 = (s32[]{:T(128)}, bf16[4,512,128]{2,1,0:T(8,128)(2,1)S(1)}, bf16[4,512,128]{2,1,0:T(8,128)(2,1)S(1)}, bf16[2560,128]{1,0:T(8,128)(2,1)S(1)}, bf16[2560,128]{1,0:T(8,128)(2,1)S(1)}, /*index=5*/s32[]{:T(128)}) while((s32[]{:T(128)}, bf16[4,512,128]{2,1,0:T(8,128)(2,1)S(1)}, bf16[4,512,128]{2,1,0:T(8,128)(2,1)S(1)}, ...), condition=%wide.region_12.12_spmd, body=%wide.region_9.11_spmd.sunk | while | flops 680328192 | bytes 17311820 | solution.py:47
  764.6 4.9 copy.56
  769.5 95.4 %all_to_all.51 = bf16[8,2048,128]{2,0,1:T(8,128)(2,1)S(1)} all-to-all(bf16[8,2048,128]{2,0,1:T(8,128)(2,1)S(1)} %copy.56), channel_id=1, replica_groups=mesh['groups'=2,'seq'=4,'adapt'=4] {'seq'}, dimensions={1} | all-to-all | bytes 8388608 | tf_op jit(solution)/shard_map/all_to_all | solution.py:119
  864.9 2.9 copy.58
  867.8 6.6 copy.59
  874.4 6.4 copy.60
  (139 shorter events, 92.5 us)
Async XLA Ops:
  7.4 1.8 copy-start
  7.4 182.9 %all-reduce.3.cloned.1.call-start = ((), (), s32[]{:S(2)}) async-start(), calls=%async_computation.4 | async-start | bytes 9437184 | tf_op jit(solution)/shard_map/psum | solution.py:86
  15.2 8.3 copy-start.2
  15.2 175.1 %all-gather.2.cloned.1.call-start = ((), (), s32[]{:S(2)}) async-start(), calls=%async_computation.3 | async-start | bytes 31457280 | tf_op jit(solution)/shard_map/all_gather | solution.py:90
  33.0 0.7 copy-start.4
  304.6 98.7 %all-to-all-start = ((bf16[32,512,128]{2,1,0:T(8,128)(2,1)}), bf16[32,512,128]{2,1,0:T(8,128)(2,1)}, u32[]{:S(2)}, u32[]{:S(2)}) async-start(bf16[32,512,128]{2,1,0:T(8,128)(2,1)} %bitcast.96), calls=%async_computation | async-start | bytes 8388608 | tf_op jit(solution)/shard_map/all_to_all | solution.py:115
  323.1 4.6 copy-start.3
  403.3 233.8 %all-to-all-start.1 = ((bf16[32,640,2,128]{3,1,2,0:T(8,128)(2,1)}), bf16[32,640,2,128]{3,1,2,0:T(8,128)(2,1)}, u32[]{:S(2)}, u32[]{:S(2)}) async-start(bf16[32,640,2,128]{3,1,2,0:T(8,128)(2,1)} %bitcast.94), calls=%async_computation.1 | async-start | bytes 20971520 | tf_op jit(solution)/shard_map/all_to_all | solution.py:116
  867.8 13.0 %copy-start.1 = (bf16[4,3072,64]{1,2,0:T(8,128)(2,1)S(1)}, bf16[4,3072,64]{1,2,0:T(8,128)(2,1)}, u32[]{:S(2)}) copy-start(bf16[4,3072,64]{1,2,0:T(8,128)(2,1)} %param.17) | copy-start | bytes 4718596
Sparse Core Ops, SparseCore 0:
  15.3 174.9 all-reduce.2
Sparse Core Ops, SparseCore 1:
  33.1 157.0 all-gather.1
where the time goes:
time: 891 us; the launch traced here: 888 us
  waiting for transfers between devices  417 us (47%)
  matrix products  141 us (16%)
  local copies, waits for them, and re-layouts  123 us (14%)
  blocking collectives  95.4 us (11%)
  other arithmetic  85 us (10%)
  between operations  15 us (2%)
  starting transfers between devices  11.2 us (1%)
    all_to_all x1, waiting for transfers between devices, on_device(): lax.all_to_all(joined, 'seq', split_axis=0, concat_axis=1, tiled=True)  223 us
    psum x1, waiting for transfers between devices, on_device(): lax.psum(up_terms, 'seq').astype(jnp.float32)  156 us
    all_to_all x1, blocking collectives, on_device(): lax.all_to_all(attended, 'seq', split_axis=1, concat_axis=0, tiled=True)  95.4 us
    dot_general x1, matrix products, on_device(): jnp.einsum('rtd,dc->rtc', block_rows, query_key_value_weight, preferred_e...  47.6 us
    all_to_all x1, waiting for transfers between devices, on_device(): lax.all_to_all(queries, 'seq', split_axis=0, concat_axis=1, tiled=True)  38.2 us
    dot_general x32, matrix products, one_block(): jnp.dot(weights.astype(jnp.bfloat16), value_rows, preferred_element_type=...  33.5 us
    dot_general x32, matrix products, one_block(): lax.dot_general(block_rows, key_rows, (((1,), (1,)), ((), ())), preferred...  29.7 us
    reduce_sum x32, other arithmetic, one_block(): weights = weights / jnp.sum(weights, axis=-1, keepdims=True)  27 us
  transfers between devices with their start and end apart: 4, of which 3 were waited for; matrix products, arithmetic and copies ran while one was open for 9% of the time, Pallas kernels for 0%

commit v1 on v0

--- a/solution.py
+++ b/solution.py
@@ -116,7 +116,9 @@
         lax.all_to_all(joined, "seq", split_axis=0, concat_axis=1, tiled=True),
     )
     attended = lax.map(attend_item, (query_items, joined_items))
-    returned = lax.all_to_all(attended, "seq", split_axis=1, concat_axis=0, tiled=True)
+    pieces = jnp.split(attended, lax.axis_size("seq"), axis=1)
+    received = lax.all_to_all(jnp.stack(pieces), "seq", 0, 0)
+    returned = jnp.concatenate(received, axis=0)
     returned = returned.reshape(all_requests, heads_local, token_local, HEAD_SIZE)
     return jnp.transpose(returned, (0, 2, 1, 3)).reshape(
         all_requests, token_local, heads_local * HEAD_SIZE

time: 891 us -> 886 us (level)
  no operation moved by 1% of the time
where the time goes in v1:
time: 886 us; the launch traced here: 883 us
  waiting for transfers between devices  417 us (47%)
  matrix products  141 us (16%)
  local copies, waits for them, and re-layouts  117 us (13%)
  blocking collectives  95.4 us (11%)
  other arithmetic  85.6 us (10%)
  between operations  15 us (2%)
  starting transfers between devices  11.2 us (1%)
    all_to_all x1, waiting for transfers between devices, on_device(): lax.all_to_all(joined, 'seq', split_axis=0, concat_axis=1, tiled=True)  223 us
    psum x1, waiting for transfers between devices, on_device(): lax.psum(up_terms, 'seq').astype(jnp.float32)  156 us
    all_to_all x1, blocking collectives, on_device(): received = lax.all_to_all(jnp.stack(pieces), 'seq', 0, 0)  95.4 us
    dot_general x1, matrix products, on_device(): jnp.einsum('rtd,dc->rtc', block_rows, query_key_value_weight, preferred_e...  47.6 us
    all_to_all x1, waiting for transfers between devices, on_device(): lax.all_to_all(queries, 'seq', split_axis=0, concat_axis=1, tiled=True)  38.2 us
    dot_general x32, matrix products, one_block(): jnp.dot(weights.astype(jnp.bfloat16), value_rows, preferred_element_type=...  33.5 us
    dot_general x32, matrix products, one_block(): lax.dot_general(block_rows, key_rows, (((1,), (1,)), ((), ())), preferred...  29.7 us
    reduce_sum x32, other arithmetic, one_block(): weights = weights / jnp.sum(weights, axis=-1, keepdims=True)  27 us
  transfers between devices with their start and end apart: 4, of which 3 were waited for; matrix products, arithmetic and copies ran while one was open for 9% of the time, Pallas kernels for 0%

profile of v1, /device:TPU:0, one launch (start us, length us, event | category | flops | bytes accessed | tf_op | source)
XLA Modules:
  0.0 883.0 jit_solution(18415514498255952773)
XLA Ops:
  9.2 2.8 convolution_convert_fusion
  12.1 3.1 convolution_convert_fusion.1
  15.2 3.7 convert_reduce_fusion
  18.9 4.5 fusion.10
  23.6 9.4 %fusion.13 = bf16[2,512,3072]{2,1,0:T(8,128)(2,1)} fusion(bf16[2,512,3072]{2,1,0:T(8,128)(2,1)} %param.14, f32[2,3072]{1,0:T(2,128)S(1)} %get-tuple-element.87, f32[2,512]{1,0:T(2,128)S(1)} %add_rsqrt_fusion.2, f32[2,512]{1,0:T(2,128)S(1)} %broadcast_multiply_fusion, f32[2,3072]{1,0:T(2,128)S(1)} %get-tuple-element.88), kind=kLoop, calls=%fused_computation.24 | loop fusion | flops 18874368 | bytes 12640256 | tf_op jit(solution)/shard_map/convert_element_type | solution.py:15
  34.2 156.1 %all-reduce.3.cloned.1.call-done = (bf16[8,64,1536]{2,0,1:T(8,128)(2,1)}, bf16[8,3072,64]{1,0,2:T(8,128)(2,1)}) async-done(((bf16[8,64,1536]{2,0,1:T(8,128)(2,1)}, bf16[8,3072,64]{1,0,2:T(8,128)(2,1)}), (bf16[8,64,1536]{2,0,1:T(8,128)(2,1)}, bf16[8,3072,64]{1,0,2:T(8,128)(2,1)})) %all-reduce.3.cloned.1.call-update) | async-done | bytes 4718608 | tf_op jit(solution)/shard_map/psum | solution.py:86
  190.3 23.9 %fusion.18 = f32[8,512,1536]{2,1,0:T(8,128)} fusion(bf16[8,64,1536]{2,0,1:T(8,128)(2,1)} %get-tuple-element.73, bf16[8,512,3072]{2,1,0:T(8,128)(2,1)} %all-gather.2.cloned.1.call-done, bf16[8,3072,64]{1,0,2:T(8,128)(2,1)} %get-tuple-element.74), kind=kOutput, calls=%fused_computation.42 | convolution fusion | flops 2416181248 | bytes 55050240 | tf_op jit(solution)/shard_map/rtk,rkc->rtc/dot_general | solution.py:97
  214.3 47.6 %convolution_add_fusion = f32[8,512,1536]{2,1,0:T(8,128)} fusion(f32[8,512,1536]{2,1,0:T(8,128)} %fusion.18, bf16[8,512,3072]{2,1,0:T(8,128)(2,1)} %all-gather.2.cloned.1.call-done, bf16[3072,1536]{1,0:T(8,128)(2,1)} %param.16), kind=kOutput, calls=%fused_computation.16 | convolution fusion | flops 38660997120 | bytes 84934656 | tf_op jit(solution)/shard_map/rtd,dc->rtc/dot_general | solution.py:94
  261.9 24.7 %copy.45 = f32[8,512,1536]{1,2,0:T(8,128)} copy(f32[8,512,1536]{2,1,0:T(8,128)} %convolution_add_fusion) | data formatting | bytes 50331648 | tf_op jit(solution)/shard_map/add | solution.py:97
  286.6 4.6 multiply_reduce_fusion.1
  291.2 7.0 fusion.15
  298.2 6.5 copy.46
  304.6 5.2 all-to-all-start
  309.8 6.2 copy.48
  316.0 3.2 copy.72
  319.1 4.0 slice.55
  323.1 4.6 multiply_reduce_fusion
  327.8 7.0 multiply_convert_fusion
  334.7 6.2 maximum_bitcast_fusion
  340.9 9.1 %pad_maximum_fusion = bf16[8,4,640,2,128]{2,4,3,1,0:T(8,128)(2,1)} fusion(bf16[8,4,128,2,128]{2,4,3,1,0:T(8,128)(2,1)} %bitcast.106, bf16[8,4,512,2,128]{2,4,3,1,0:T(8,128)(2,1)} %maximum_bitcast_fusion), kind=kLoop, calls=%fused_computation.25 | loop fusion | flops 20971520 | bytes 20971520 | tf_op jit(solution)/shard_map/concatenate | solution.py:109
  350.1 15.1 %copy.50 = bf16[8,4,640,2,128]{4,2,3,1,0:T(8,128)(2,1)} copy(bf16[8,4,640,2,128]{2,4,3,1,0:T(8,128)(2,1)} %pad_maximum_fusion) | data formatting | bytes 20971520 | tf_op jit(solution)/shard_map/concatenate | solution.py:109
  365.2 38.2 %all-to-all-done = bf16[32,512,128]{2,1,0:T(8,128)(2,1)} async-done(((bf16[32,512,128]{2,1,0:T(8,128)(2,1)}), bf16[32,512,128]{2,1,0:T(8,128)(2,1)}, u32[]{:S(2)}, u32[]{:S(2)}) %all-to-all-start) | async-done | bytes 4194336 | tf_op jit(solution)/shard_map/all_to_all | solution.py:115
  403.3 6.0 all-to-all-start.1
  409.4 4.6 copy.47
  414.0 223.2 %all-to-all-done.1 = bf16[32,640,2,128]{3,1,2,0:T(8,128)(2,1)} async-done(((bf16[32,640,2,128]{3,1,2,0:T(8,128)(2,1)}), bf16[32,640,2,128]{3,1,2,0:T(8,128)(2,1)}, u32[]{:S(2)}, u32[]{:S(2)}) %all-to-all-start.1) | async-done | bytes 10485792 | tf_op jit(solution)/shard_map/all_to_all | solution.py:116
  637.1 9.2 %copy.51 = bf16[8,4,640,2,128]{4,2,1,3,0:T(8,128)(2,1)} copy(bf16[8,4,640,2,128]{4,2,3,0,1:T(8,128)(2,1)} %bitcast.23) | data formatting | bytes 20971520 | tf_op jit(solution)/shard_map/all_to_all | solution.py:116
  646.3 118.3 %while.21 = (s32[]{:T(128)}, bf16[8,2048,128]{2,1,0:T(8,128)(2,1)}, bf16[8,2048,128]{2,1,0:T(8,128)(2,1)}, bf16[8,2560,2,128]{3,1,2,0:T(8,128)(2,1)}, s32[]{:T(128)}, /*index=5*/s32[]{:T(128)}, s32[]{:T(128)}) while((s32[]{:T(128)}, bf16[8,2048,128]{2,1,0:T(8,128)(2,1)}, bf16[8,2048,128]{2,1,0:T(8,128)(2,1)}, ...), condition=%wide.region_13.14_spmd, body=%wide.region_8.13_spmd.sunk | while | flops 680328192 | bytes 24652504 | solution.py:118
  646.3 1.4 dynamic-slice_bitcast_fusion.2
  647.8 1.1 constant_dynamic-slice_fusion.2
  648.9 11.3 %while.22 = (s32[]{:T(128)}, bf16[4,512,128]{2,1,0:T(8,128)(2,1)S(1)}, bf16[4,512,128]{2,1,0:T(8,128)(2,1)S(1)}, bf16[2560,128]{1,0:T(8,128)(2,1)S(1)}, bf16[2560,128]{1,0:T(8,128)(2,1)S(1)}, /*index=5*/s32[]{:T(128)}) while((s32[]{:T(128)}, bf16[4,512,128]{2,1,0:T(8,128)(2,1)S(1)}, bf16[4,512,128]{2,1,0:T(8,128)(2,1)S(1)}, ...), condition=%wide.region_12.12_spmd, body=%wide.region_9.11_spmd.sunk | while | flops 680328192 | bytes 17311820 | solution.py:47
  653.6 1.0 fusion.46
  656.4 1.0 fusion.46
  659.2 1.0 fusion.46
  661.1 1.4 dynamic-slice_bitcast_fusion.2
  662.6 1.1 constant_dynamic-slice_fusion.2
  663.7 11.4 %while.22 = (s32[]{:T(128)}, bf16[4,512,128]{2,1,0:T(8,128)(2,1)S(1)}, bf16[4,512,128]{2,1,0:T(8,128)(2,1)S(1)}, bf16[2560,128]{1,0:T(8,128)(2,1)S(1)}, bf16[2560,128]{1,0:T(8,128)(2,1)S(1)}, /*index=5*/s32[]{:T(128)}) while((s32[]{:T(128)}, bf16[4,512,128]{2,1,0:T(8,128)(2,1)S(1)}, bf16[4,512,128]{2,1,0:T(8,128)(2,1)S(1)}, ...), condition=%wide.region_12.12_spmd, body=%wide.region_9.11_spmd.sunk | while | flops 680328192 | bytes 17311820 | solution.py:47
  668.3 1.0 fusion.46
  671.2 1.0 fusion.46
  674.0 1.0 fusion.46
  675.9 1.4 dynamic-slice_bitcast_fusion.2
  677.4 1.1 constant_dynamic-slice_fusion.2
  678.5 11.4 %while.22 = (s32[]{:T(128)}, bf16[4,512,128]{2,1,0:T(8,128)(2,1)S(1)}, bf16[4,512,128]{2,1,0:T(8,128)(2,1)S(1)}, bf16[2560,128]{1,0:T(8,128)(2,1)S(1)}, bf16[2560,128]{1,0:T(8,128)(2,1)S(1)}, /*index=5*/s32[]{:T(128)}) while((s32[]{:T(128)}, bf16[4,512,128]{2,1,0:T(8,128)(2,1)S(1)}, bf16[4,512,128]{2,1,0:T(8,128)(2,1)S(1)}, ...), condition=%wide.region_12.12_spmd, body=%wide.region_9.11_spmd.sunk | while | flops 680328192 | bytes 17311820 | solution.py:47
  680.3 1.0 fusion.46
  683.1 1.0 fusion.46
  686.0 1.0 fusion.46
  690.7 1.4 dynamic-slice_bitcast_fusion.2
  692.2 1.1 constant_dynamic-slice_fusion.2
  693.3 11.4 %while.22 = (s32[]{:T(128)}, bf16[4,512,128]{2,1,0:T(8,128)(2,1)S(1)}, bf16[4,512,128]{2,1,0:T(8,128)(2,1)S(1)}, bf16[2560,128]{1,0:T(8,128)(2,1)S(1)}, bf16[2560,128]{1,0:T(8,128)(2,1)S(1)}, /*index=5*/s32[]{:T(128)}) while((s32[]{:T(128)}, bf16[4,512,128]{2,1,0:T(8,128)(2,1)S(1)}, bf16[4,512,128]{2,1,0:T(8,128)(2,1)S(1)}, ...), condition=%wide.region_12.12_spmd, body=%wide.region_9.11_spmd.sunk | while | flops 680328192 | bytes 17311820 | solution.py:47
  705.5 1.4 dynamic-slice_bitcast_fusion.2
  707.0 1.1 constant_dynamic-slice_fusion.2
  708.1 11.4 %while.22 = (s32[]{:T(128)}, bf16[4,512,128]{2,1,0:T(8,128)(2,1)S(1)}, bf16[4,512,128]{2,1,0:T(8,128)(2,1)S(1)}, bf16[2560,128]{1,0:T(8,128)(2,1)S(1)}, bf16[2560,128]{1,0:T(8,128)(2,1)S(1)}, /*index=5*/s32[]{:T(128)}) while((s32[]{:T(128)}, bf16[4,512,128]{2,1,0:T(8,128)(2,1)S(1)}, bf16[4,512,128]{2,1,0:T(8,128)(2,1)S(1)}, ...), condition=%wide.region_12.12_spmd, body=%wide.region_9.11_spmd.sunk | while | flops 680328192 | bytes 17311820 | solution.py:47
  720.3 1.4 dynamic-slice_bitcast_fusion.2
  721.8 1.1 constant_dynamic-slice_fusion.2
  722.9 11.4 %while.22 = (s32[]{:T(128)}, bf16[4,512,128]{2,1,0:T(8,128)(2,1)S(1)}, bf16[4,512,128]{2,1,0:T(8,128)(2,1)S(1)}, bf16[2560,128]{1,0:T(8,128)(2,1)S(1)}, bf16[2560,128]{1,0:T(8,128)(2,1)S(1)}, /*index=5*/s32[]{:T(128)}) while((s32[]{:T(128)}, bf16[4,512,128]{2,1,0:T(8,128)(2,1)S(1)}, bf16[4,512,128]{2,1,0:T(8,128)(2,1)S(1)}, ...), condition=%wide.region_12.12_spmd, body=%wide.region_9.11_spmd.sunk | while | flops 680328192 | bytes 17311820 | solution.py:47
  735.1 1.4 dynamic-slice_bitcast_fusion.2
  736.6 1.1 constant_dynamic-slice_fusion.2
  737.6 11.4 %while.22 = (s32[]{:T(128)}, bf16[4,512,128]{2,1,0:T(8,128)(2,1)S(1)}, bf16[4,512,128]{2,1,0:T(8,128)(2,1)S(1)}, bf16[2560,128]{1,0:T(8,128)(2,1)S(1)}, bf16[2560,128]{1,0:T(8,128)(2,1)S(1)}, /*index=5*/s32[]{:T(128)}) while((s32[]{:T(128)}, bf16[4,512,128]{2,1,0:T(8,128)(2,1)S(1)}, bf16[4,512,128]{2,1,0:T(8,128)(2,1)S(1)}, ...), condition=%wide.region_12.12_spmd, body=%wide.region_9.11_spmd.sunk | while | flops 680328192 | bytes 17311820 | solution.py:47
  749.8 1.4 dynamic-slice_bitcast_fusion.2
  751.3 1.1 constant_dynamic-slice_fusion.2
  752.4 11.4 %while.22 = (s32[]{:T(128)}, bf16[4,512,128]{2,1,0:T(8,128)(2,1)S(1)}, bf16[4,512,128]{2,1,0:T(8,128)(2,1)S(1)}, bf16[2560,128]{1,0:T(8,128)(2,1)S(1)}, bf16[2560,128]{1,0:T(8,128)(2,1)S(1)}, /*index=5*/s32[]{:T(128)}) while((s32[]{:T(128)}, bf16[4,512,128]{2,1,0:T(8,128)(2,1)S(1)}, bf16[4,512,128]{2,1,0:T(8,128)(2,1)S(1)}, ...), condition=%wide.region_12.12_spmd, body=%wide.region_9.11_spmd.sunk | while | flops 680328192 | bytes 17311820 | solution.py:47
  764.6 2.6 slice_bitcast_fusion.6
  767.8 95.4 %all_to_all.41 = bf16[4,8,512,128]{3,2,1,0:T(8,128)(2,1)S(1)} all-to-all(bf16[4,8,512,128]{3,2,1,0:T(8,128)(2,1)S(1)} %pad_maximum_fusion.1), channel_id=1, replica_groups=mesh['groups'=2,'seq'=4,'adapt'=4] {'seq'}, dimensions={0} | all-to-all | bytes 8388608 | tf_op jit(solution)/shard_map/all_to_all | solution.py:120
  863.2 5.2 copy.71
  868.4 7.2 reshape.93
  (139 shorter events, 92.0 us)
Async XLA Ops:
  7.4 1.8 copy-start
  7.4 182.9 %all-reduce.3.cloned.1.call-start = ((), (), s32[]{:S(2)}) async-start(), calls=%async_computation.4 | async-start | bytes 9437184 | tf_op jit(solution)/shard_map/psum | solution.py:86
  15.2 8.3 copy-start.2
  15.2 175.1 %all-gather.2.cloned.1.call-start = ((), (), s32[]{:S(2)}) async-start(), calls=%async_computation.3 | async-start | bytes 31457280 | tf_op jit(solution)/shard_map/all_gather | solution.py:90
  33.0 0.7 copy-start.4
  304.6 98.7 %all-to-all-start = ((bf16[32,512,128]{2,1,0:T(8,128)(2,1)}), bf16[32,512,128]{2,1,0:T(8,128)(2,1)}, u32[]{:S(2)}, u32[]{:S(2)}) async-start(bf16[32,512,128]{2,1,0:T(8,128)(2,1)} %bitcast.101), calls=%async_computation | async-start | bytes 8388608 | tf_op jit(solution)/shard_map/all_to_all | solution.py:115
  323.1 4.6 copy-start.3
  403.3 233.8 %all-to-all-start.1 = ((bf16[32,640,2,128]{3,1,2,0:T(8,128)(2,1)}), bf16[32,640,2,128]{3,1,2,0:T(8,128)(2,1)}, u32[]{:S(2)}, u32[]{:S(2)}) async-start(bf16[32,640,2,128]{3,1,2,0:T(8,128)(2,1)} %bitcast.99), calls=%async_computation.1 | async-start | bytes 20971520 | tf_op jit(solution)/shard_map/all_to_all | solution.py:116
  863.2 12.3 %copy-start.1 = (bf16[4,3072,64]{1,2,0:T(8,128)(2,1)S(1)}, bf16[4,3072,64]{1,2,0:T(8,128)(2,1)}, u32[]{:S(2)}) copy-start(bf16[4,3072,64]{1,2,0:T(8,128)(2,1)} %param.17) | copy-start | bytes 4718596
Sparse Core Ops, SparseCore 0:
  15.3 174.9 all-reduce.2
Sparse Core Ops, SparseCore 1:
  33.1 157.0 all-gather.1
